TPU v7x, 256 devices: a whole 4x4x8 slice. The times are simulated.
256 devices in a mesh: ctx: 64 (over z, y, core), ch: 4 (over x).
Axes of the slice: x: 4, y: 4, z: 8, core: 2. Of those that a mesh axis runs over, the one named last changes fastest.
Arguments:
- conv_input: bfloat16 [256, 128, 8192], P('ctx', None, 'ch'), may hold values from -6 to 6
- gate_signal: bfloat16 [256, 128, 8192], P('ctx', None, 'ch'), may hold values from -6 to 6
- cotangent: bfloat16 [256, 128, 8192], P('ctx', None, 'ch'), may hold values from -6 to 6
- filters: float32 [16, 1024], replicated
- tile_owner: int32 [192], replicated, may hold values from 0 to 63, as said below
- support: int32 [192, 8], replicated, may hold values from -1 to 191, as said below
Outputs:
- gate_grad: bfloat16 [256, 128, 8192], P('ctx', None, 'ch')
- input_grad: bfloat16 [256, 128, 8192], P('ctx', None, 'ch')
- filter_grad: float32 [16, 1024], replicated
Inputs may be any that keep to these rules, and one draw needn't show every extreme that they name: tile_owner never falls from one tile to the next; every index of ctx owns from 2 to 4 tiles, some index owns 3 + 1 and some index owns 3 - 1. support[t, k] is t - k where tile t - k belongs to the document of tile t and -1 otherwise; documents are runs of whole tiles, and some document spans 8 tiles or more.
All inputs are finite; a program needn't handle non-finite values.
Results may differ from a plain program's by a relative error of at most 0.0058.
Values may be sent and summed in bfloat16 or wider, within the bound.
No kernel may reach another device: no remote copies, remote signals or barrier semaphores. Data moves between devices by JAX's collectives and lax.ppermute only.
A program may use at most 256 MiB of HBM per device.

v0:
```python
import math
import jax
import jax.numpy as jnp
from jax import lax
from jax.sharding import PartitionSpec as P

GROUP = 128
REACH = 4


def passed_along(value, axis, steps):
    count = lax.axis_size(axis)
    leading, last = (max(0, -steps), min(count, count - steps))
    return lax.ppermute(value, axis, [(source, source + steps) for source in range(leading, last)])


def filter_blocks(filters, tile_rows, maxlag):
    narrow = filters.astype(jnp.bfloat16)
    row_ids = jnp.arange(tile_rows, dtype=jnp.int32)
    lag_offsets = (
        jnp.arange(maxlag, dtype=jnp.int32)[:, None, None] * tile_rows
        + row_ids[:, None]
        - row_ids[None, :]
    )
    picked = jnp.take(narrow, jnp.clip(lag_offsets, 0, filters.shape[1] - 1), axis=1)
    return jnp.where(lag_offsets[None] >= 0, picked, jnp.zeros_like(picked))


def lag_sums(square):
    filter_count, side_length = (square.shape[0], square.shape[1])
    flipped = square[:, :, ::-1]
    padded = jnp.pad(flipped, ((0, 0), (0, 0), (0, side_length)))
    skewed = padded.reshape(filter_count, 2 * side_length * side_length)[
        :, : side_length * (2 * side_length - 1)
    ]
    return jnp.sum(skewed.reshape(filter_count, side_length, 2 * side_length - 1), axis=1)


def spread_lags(squares, lag_count):
    maxlag, filter_count, side_length = (squares.shape[0], squares.shape[1], squares.shape[2])
    accumulated = jnp.zeros((filter_count, (maxlag + 1) * side_length), jnp.float32)
    for lag_index in range(maxlag):
        start_col = lag_index * side_length
        accumulated = accumulated.at[:, start_col : start_col + 2 * side_length - 1].add(
            lag_sums(squares[lag_index])
        )
    return accumulated[:, side_length - 1 : side_length - 1 + lag_count]


def per_device(conv_input, gate_signal, cotangent, filters, tile_owner, support):
    slot_count, tile_rows, channels = conv_input.shape
    maxlag = support.shape[1]
    filter_count, lag_count = filters.shape
    group_width = GROUP
    repeats = channels // (filter_count * group_width)
    total_tiles = tile_owner.shape[0]
    devices_ctx = lax.axis_size("ctx")
    myself = lax.axis_index("ctx")
    farthest = REACH
    devices = jnp.arange(devices_ctx, dtype=jnp.int32)
    counts = jnp.sum((tile_owner[None, :] == devices[:, None]).astype(jnp.int32), axis=1)
    starts = jnp.cumsum(counts) - counts
    slot_index = jnp.arange(slot_count, dtype=jnp.int32)
    own_tiles = starts[myself] + slot_index
    own_live = slot_index < counts[myself]
    own_safe = jnp.clip(own_tiles, 0, total_tiles - 1)
    sources = support[own_safe]
    present = own_live[:, None] & (sources >= 0)
    source_safe = jnp.clip(sources, 0, total_tiles - 1)
    holder = tile_owner[source_safe]
    within = source_safe - starts[holder]
    blocks = filter_blocks(filters, tile_rows, maxlag)
    zero_tile = jnp.zeros((), jnp.bfloat16)
    gathered = [conv_input]
    for distance in range(1, farthest + 1):
        gathered.append(passed_along(conv_input, "ctx", distance))
    window = jnp.concatenate(gathered, axis=0)
    rows_at = jnp.clip((myself - holder) * slot_count + within, 0, window.shape[0] - 1)
    selected = jnp.take(window, rows_at.reshape(-1), axis=0)
    selected = selected.reshape(slot_count, maxlag, tile_rows, channels)
    selected = jnp.where(present[:, :, None, None], selected, zero_tile)
    weighted = (gate_signal.astype(jnp.float32) * cotangent.astype(jnp.float32)).astype(
        jnp.bfloat16
    )
    weighted = jnp.where(own_live[:, None, None], weighted, zero_tile)
    weighted_shaped = weighted.reshape(slot_count, tile_rows, repeats, filter_count, group_width)
    conv_out = jnp.zeros((slot_count, tile_rows, channels), jnp.float32)
    squares = []
    for lag_index in range(maxlag):
        shaped = selected[:, lag_index].reshape(
            slot_count, tile_rows, repeats, filter_count, group_width
        )
        product = jnp.einsum(
            "fij,sjrfc->sirfc", blocks[:, lag_index], shaped, preferred_element_type=jnp.float32
        )
        conv_out = conv_out + product.reshape(slot_count, tile_rows, channels)
        squares.append(
            jnp.einsum(
                "sirfc,sjrfc->fij", weighted_shaped, shaped, preferred_element_type=jnp.float32
            )
        )
    gate_grad = (cotangent.astype(jnp.float32) * conv_out).astype(jnp.bfloat16)
    norm_factor = 1.0 / math.sqrt(
        total_tiles * tile_rows * channels * lax.axis_size("ch") / filter_count
    )
    local_filters = spread_lags(jnp.stack(squares), lag_count)
    filter_grad = lax.psum(local_filters, ("ctx", "ch")) * norm_factor
    row_count = (farthest + 1) * slot_count
    partial_value = jnp.zeros((row_count, tile_rows, channels), jnp.float32)
    back_rows = jnp.clip((myself - holder) * slot_count + within, 0, row_count - 1)
    for lag_index in range(maxlag):
        adjoint_term = jnp.einsum(
            "fji,sjrfc->sirfc",
            blocks[:, lag_index],
            weighted_shaped,
            preferred_element_type=jnp.float32,
        )
        adjoint_term = jnp.where(present[:, lag_index, None, None, None, None], adjoint_term, 0.0)
        partial_value = partial_value.at[back_rows[:, lag_index]].add(
            adjoint_term.reshape(slot_count, tile_rows, channels)
        )
    adjoint = partial_value[:slot_count]
    for distance in range(1, farthest + 1):
        adjoint = adjoint + passed_along(
            partial_value[distance * slot_count : (distance + 1) * slot_count], "ctx", -distance
        )
    input_grad = adjoint.astype(jnp.bfloat16)
    return (gate_grad, input_grad, filter_grad)


def solution(mesh):
    return jax.shard_map(
        per_device,
        mesh=mesh,
        in_specs=(P("ctx", None, "ch"), P("ctx", None, "ch"), P("ctx", None, "ch"), P(), P(), P()),
        out_specs=(P("ctx", None, "ch"), P("ctx", None, "ch"), P()),
        check_vma=False,
    )
```

profile of v0, /device:TPU:1, one launch (start us, length us, event | category | flops | bytes accessed | tf_op | source)
XLA Modules:
  0.0 1289.1 jit_solution(6269767289445348876)
XLA Ops:
  32.1 454.0 %gather_fusion.4 = bf16[131072,16]{1,0:T(8,128)(2,1)} fusion(bf16[16,1024]{0,1:T(8,128)(2,1)S(1)} %copy.164, s32[131072]{0:T(1024)S(1)} %broadcast_clamp_fusion), kind=kCustom, calls=%fused_computation.4 | custom fusion | bytes 8912896 | tf_op jit(solution)/shard_map/jit(_take)/gather | solution.py:25
  486.1 29.2 %copy.166 = bf16[8,128,128,16]{2,1,3,0:T(8,128)(2,1)} copy(bf16[8,128,128,16]{3,2,1,0:T(8,128)(2,1)} %bitcast.207) | data formatting | bytes 8388608 | tf_op jit(solution)/shard_map/jit(_take)/gather | solution.py:25
  547.7 5.4 copy.186
  553.1 4.7 copy.188
  557.7 5.4 copy.189
  563.1 4.7 copy.191
  567.8 5.4 copy.192
  573.2 4.7 copy.194
  577.8 5.4 copy.195
  583.2 4.7 copy.197
  587.9 5.4 copy.198
  593.3 4.7 copy.200
  598.0 5.6 copy.201
  603.5 4.7 copy.203
  608.2 5.4 copy.204
  618.2 5.4 copy.207
  623.9 9.7 broadcast_in_dim.155
  633.6 9.0 scatter_fusion
  642.5 9.0 scatter_fusion.1
  651.6 9.0 scatter_fusion.2
  660.6 9.0 scatter_fusion.3
  669.6 8.7 scatter_fusion.4
  678.3 8.6 scatter_fusion.5
  686.9 8.3 scatter_fusion.6
  695.1 8.3 scatter_fusion.7
  703.4 12.2 fusion.52
  742.8 11.4 gather_fusion.3
  754.2 8.7 select_select_fusion
  762.9 5.9 fusion.53
  836.1 11.8 add_bitcast_fusion
  850.1 9.3 rev.24
  863.5 6.2 reshape.668
  872.1 9.3 rev.25
  885.6 6.2 reshape.670
  893.5 6.0 rev.26
  903.6 6.2 reshape.672
  913.9 5.8 rev.27
  923.8 6.2 reshape.674
  934.1 6.0 rev.28
  944.3 6.2 reshape.676
  954.6 5.8 rev.29
  964.5 6.2 reshape.678
  974.8 6.1 rev.30
  985.0 6.2 reshape.680
  995.3 5.8 rev.31
  1005.2 6.3 reshape.682
  1028.9 241.1 %all-reduce.11.cloned.1.call-done = f32[16,1024]{1,0:T(8,128)} async-done(((f32[16,1024]{1,0:T(8,128)}), f32[16,1024]{1,0:T(8,128)}) %all-reduce.11.cloned.1.call-update) | async-done | bytes 65552 | tf_op jit(solution)/shard_map/psum | solution.py:107
  1271.5 10.4 fusion.5
  (174 shorter events, 234.9 us)
Async XLA Ops:
  7.2 24.7 %copy-start.7 = (f32[16,1024]{1,0:T(8,128)S(1)}, f32[16,1024]{1,0:T(8,128)}, u32[]{:S(2)}) copy-start(f32[16,1024]{1,0:T(8,128)} %param.25) | copy-start | bytes 196612
  7.2 1262.8 %all-reduce.11.cloned.1.call-start = ((), (), s32[]{:S(2)}) async-start(), calls=%async_computation | async-start | bytes 131072 | tf_op jit(solution)/shard_map/psum | solution.py:107
  7.2 718.4 %collective-permute-start = (bf16[4,128,2048]{2,1,0:T(8,128)(2,1)}, bf16[4,128,2048]{2,1,0:T(8,128)(2,1)}, u32[]{:S(2)}, u32[]{:S(2)}) collective-permute-start(bf16[4,128,2048]{2,1,0:T(8,128)(2,1)} %param.22), channel_id=1, source_target_pairs={{0,4},{4,8},{8,12},{12,16},{16,20},{20,24},{24,28},{28,32},{32,36}... | collective-permute-start | bytes 6291464 | tf_op jit(solution)/shard_map/ppermute | solution.py:14
  11.8 718.2 %collective-permute-start.1 = (bf16[4,128,2048]{2,1,0:T(8,128)(2,1)}, bf16[4,128,2048]{2,1,0:T(8,128)(2,1)}, u32[]{:S(2)}, u32[]{:S(2)}) collective-permute-start(bf16[4,128,2048]{2,1,0:T(8,128)(2,1)} %param.22), channel_id=1, source_target_pairs={{0,8},{4,12},{8,16},{12,20},{16,24},{20,28},{24,32},{28,36},{32,40... | collective-permute-start | bytes 6291464 | tf_op jit(solution)/shard_map/ppermute | solution.py:14
  16.3 718.2 %collective-permute-start.2 = (bf16[4,128,2048]{2,1,0:T(8,128)(2,1)}, bf16[4,128,2048]{2,1,0:T(8,128)(2,1)}, u32[]{:S(2)}, u32[]{:S(2)}) collective-permute-start(bf16[4,128,2048]{2,1,0:T(8,128)(2,1)} %param.22), channel_id=1, source_target_pairs={{0,12},{4,16},{8,20},{12,24},{16,28},{20,32},{24,36},{28,40},{32,4... | collective-permute-start | bytes 6291464 | tf_op jit(solution)/shard_map/ppermute | solution.py:14
  19.9 719.7 %collective-permute-start.3 = (bf16[4,128,2048]{2,1,0:T(8,128)(2,1)}, bf16[4,128,2048]{2,1,0:T(8,128)(2,1)}, u32[]{:S(2)}, u32[]{:S(2)}) collective-permute-start(bf16[4,128,2048]{2,1,0:T(8,128)(2,1)} %param.22), channel_id=1, source_target_pairs={{0,16},{4,20},{8,24},{12,28},{16,32},{20,36},{24,40},{28,44},{32,4... | collective-permute-start | bytes 6291464 | tf_op jit(solution)/shard_map/ppermute | solution.py:14
  486.1 29.2 %copy-start.6 = (bf16[4,128,2048]{2,1,0:T(8,128)(2,1)S(1)}, bf16[4,128,2048]{2,1,0:T(8,128)(2,1)}, u32[]{:S(2)}) copy-start(bf16[4,128,2048]{2,1,0:T(8,128)(2,1)} %param.24) | copy-start | bytes 6291460
  522.1 3.4 copy-start.5
  526.1 16.7 %copy-start = (bf16[16,8,128,128]{3,2,0,1:T(8,128)(2,1)}, bf16[16,8,128,128]{3,2,0,1:T(8,128)(2,1)S(1)}, u32[]{:S(2)}) copy-start(bf16[16,8,128,128]{3,2,0,1:T(8,128)(2,1)S(1)} %select_bitcast_fusion) | copy-start | bytes 12582916
  715.7 555.8 %collective-permute-start.7 = (f32[4,128,2048]{2,1,0:T(8,128)}, f32[4,128,2048]{2,1,0:T(8,128)}, u32[]{:S(2)}, u32[]{:S(2)}) collective-permute-start(f32[4,128,2048]{2,1,0:T(8,128)} %get-tuple-element.127), channel_id=1, source_target_pairs={{16,0},{20,4},{24,8},{28,12},{32,16},{36,20},{40,24},{44,28},{48,3... | collective-permute-start | bytes 12582920 | tf_op jit(solution)/shard_map/ppermute | solution.py:14
  725.6 545.8 %collective-permute-start.6 = (f32[4,128,2048]{2,1,0:T(8,128)}, f32[4,128,2048]{2,1,0:T(8,128)}, u32[]{:S(2)}, u32[]{:S(2)}) collective-permute-start(f32[4,128,2048]{2,1,0:T(8,128)} %get-tuple-element.128), channel_id=1, source_target_pairs={{12,0},{16,4},{20,8},{24,12},{28,16},{32,20},{36,24},{40,28},{44,3... | collective-permute-start | bytes 12582920 | tf_op jit(solution)/shard_map/ppermute | solution.py:14
  730.0 541.4 %collective-permute-start.5 = (f32[4,128,2048]{2,1,0:T(8,128)}, f32[4,128,2048]{2,1,0:T(8,128)}, u32[]{:S(2)}, u32[]{:S(2)}) collective-permute-start(f32[4,128,2048]{2,1,0:T(8,128)} %get-tuple-element.129), channel_id=1, source_target_pairs={{8,0},{12,4},{16,8},{20,12},{24,16},{28,20},{32,24},{36,28},{40,32... | collective-permute-start | bytes 12582920 | tf_op jit(solution)/shard_map/ppermute | solution.py:14
  734.5 536.9 %collective-permute-start.4 = (f32[4,128,2048]{2,1,0:T(8,128)}, f32[4,128,2048]{2,1,0:T(8,128)}, u32[]{:S(2)}, u32[]{:S(2)}) collective-permute-start(f32[4,128,2048]{2,1,0:T(8,128)} %get-tuple-element.126), channel_id=1, source_target_pairs={{4,0},{8,4},{12,8},{16,12},{20,16},{24,20},{28,24},{32,28},{36,32}... | collective-permute-start | bytes 12582920 | tf_op jit(solution)/shard_map/ppermute | solution.py:14
  772.8 4.5 copy-start.2
  783.0 4.5 copy-start.3
  793.2 4.5 copy-start.4
  1005.2 15.8 %copy-start.1 = (bf16[4,128,2048]{1,2,0:T(8,128)(2,1)S(1)}, bf16[4,128,2048]{1,2,0:T(8,128)(2,1)}, u32[]{:S(2)}) copy-start(bf16[4,128,2048]{1,2,0:T(8,128)(2,1)} %copy.160) | copy-start | bytes 6291460
Sparse Core Ops, SparseCore 0:
  1021.1 248.8 all-reduce.10
where the time goes:
time: 1300 us; the launch traced here: 1290 us
  local copies, waits for them, and re-layouts  807 us (62%)
  waiting for transfers between devices  241 us (19%)
  other arithmetic  126 us (10%)
  matrix products  78 us (6%)
  starting transfers between devices  22.1 us (2%)
  between operations  15.1 us (1%)
    gather x2, local copies, waits for them, and re-layouts, filter_blocks(): jnp.take(narrow, jnp.clip(lag_offsets, 0, filters.shape[1] - 1), axis=1)  483 us
    psum x1, waiting for transfers between devices, per_device(): filter_grad = lax.psum(local_filters, ('ctx', 'ch')) * norm_factor  241 us
    scatter-add x8, other arithmetic, per_device(): partial_value.at[back_rows[:, lag_index]]  69.9 us
    rev x8, local copies, waits for them, and re-layouts, lag_sums(): flipped = square[:, :, ::-1]  54.3 us
    reshape x8, local copies, waits for them, and re-layouts, lag_sums(): skewed.reshape(filter_count, side_length, 2 * side_length - 1)  49.4 us
    reshape x8, local copies, waits for them, and re-layouts, per_device(): adjoint_term.reshape(slot_count, tile_rows, channels)  43.4 us
    dot_general x8, matrix products, per_device(): jnp.einsum('fij,sjrfc->sirfc', blocks[:, lag_index], shaped, preferred_el...  42.7 us
    slice x9, local copies, waits for them, and re-layouts, per_device(): selected[:, lag_index]  37.9 us
  transfers between devices with their start and end apart: 9, of which 1 were waited for; matrix products, arithmetic and copies ran while one was open for 78% of the time, Pallas kernels for 0%

commit v1 on v0

--- a/solution.py
+++ b/solution.py
@@ -6,6 +6,11 @@
 
 GROUP = 128
 REACH = 4
+
+
+def _render_blocks(vals, chip_axis):
+    local_next = jnp.sum(lax.all_gather(vals, chip_axis), 0)
+    return local_next
 
 
 def passed_along(value, axis, steps):
@@ -104,7 +109,7 @@
         total_tiles * tile_rows * channels * lax.axis_size("ch") / filter_count
     )
     local_filters = spread_lags(jnp.stack(squares), lag_count)
-    filter_grad = lax.psum(local_filters, ("ctx", "ch")) * norm_factor
+    filter_grad = _render_blocks(local_filters, ("ctx", "ch")) * norm_factor
     row_count = (farthest + 1) * slot_count
     partial_value = jnp.zeros((row_count, tile_rows, channels), jnp.float32)
     back_rows = jnp.clip((myself - holder) * slot_count + within, 0, row_count - 1)

time: 1300 us -> 1470 us (1.13)
  the two profiles are of different devices: /device:TPU:1 before, /device:TPU:99 now
where the time goes in v1:
time: 1470 us; the launch traced here: 1460 us
  local copies, waits for them, and re-layouts  779 us (53%)
  waiting for transfers between devices  383 us (26%)
  other arithmetic  131 us (9%)
  starting transfers between devices  87.1 us (6%)
  matrix products  61.5 us (4%)
  between operations  15.1 us (1%)
    gather x2, local copies, waits for them, and re-layouts, filter_blocks(): jnp.take(narrow, jnp.clip(lag_offsets, 0, filters.shape[1] - 1), axis=1)  483 us
    ppermute x8, waiting for transfers between devices, passed_along(): lax.ppermute(value, axis, [(source, source + steps) for source in range(l...  383 us
    ppermute x8, starting transfers between devices, passed_along(): lax.ppermute(value, axis, [(source, source + steps) for source in range(l...  87 us
    scatter-add x8, other arithmetic, per_device(): partial_value.at[back_rows[:, lag_index]]  70.8 us
    reshape x8, local copies, waits for them, and re-layouts, lag_sums(): skewed.reshape(filter_count, side_length, 2 * side_length - 1)  49.2 us
    rev x8, local copies, waits for them, and re-layouts, lag_sums(): flipped = square[:, :, ::-1]  47.9 us
    reshape x8, local copies, waits for them, and re-layouts, per_device(): adjoint_term.reshape(slot_count, tile_rows, channels)  43.3 us
    slice x9, local copies, waits for them, and re-layouts, per_device(): selected[:, lag_index]  37.5 us
  transfers between devices with their start and end apart: 9, of which 6 were waited for; matrix products, arithmetic and copies ran while one was open for 50% of the time, Pallas kernels for 0%

profile of v1, /device:TPU:99, one launch (start us, length us, event | category | flops | bytes accessed | tf_op | source)
XLA Modules:
  0.0 1456.9 jit_solution(13110668147050535586)
XLA Ops:
  45.3 9.0 collective-permute-done
  57.4 111.9 %collective-permute-done.1 = bf16[4,128,2048]{2,1,0:T(8,128)(2,1)} collective-permute-done((bf16[4,128,2048]{2,1,0:T(8,128)(2,1)}, bf16[4,128,2048]{2,1,0:T(8,128)(2,1)}, u32[]{:S(2)}, u32[]{:S(2)}) %collective-permute-start.1) | collective-permute-done | bytes 2097184 | tf_op jit(solution)/shard_map/ppermute | solution.py:19
  180.9 11.1 gather_fusion.3
  192.0 8.7 select_select_fusion
  200.7 5.9 fusion.53
  240.5 5.8 rev.24
  250.5 6.2 reshape.668
  261.5 6.3 rev.25
  271.9 6.2 reshape.670
  282.2 5.8 rev.26
  292.2 6.2 reshape.672
  302.4 6.0 rev.27
  312.6 6.2 reshape.674
  322.8 5.8 rev.28
  332.8 6.2 reshape.676
  343.1 6.0 rev.29
  353.3 6.2 reshape.678
  363.6 5.8 rev.30
  373.6 6.2 reshape.680
  383.8 6.2 rev.31
  394.2 6.2 reshape.682
  410.4 454.0 %gather_fusion.4 = bf16[131072,16]{1,0:T(8,128)(2,1)} fusion(bf16[16,1024]{0,1:T(8,128)(2,1)S(1)} %copy.164, s32[131072]{0:T(1024)S(1)} %broadcast_clamp_fusion), kind=kCustom, calls=%fused_computation.4 | custom fusion | bytes 8912896 | tf_op jit(solution)/shard_map/jit(_take)/gather | solution.py:30
  864.4 29.0 %copy.166 = bf16[8,128,128,16]{2,1,3,0:T(8,128)(2,1)} copy(bf16[8,128,128,16]{3,2,1,0:T(8,128)(2,1)} %bitcast.208) | data formatting | bytes 8388608 | tf_op jit(solution)/shard_map/jit(_take)/gather | solution.py:30
  902.7 5.4 copy.186
  912.0 5.4 copy.189
  921.4 5.5 copy.192
  930.9 5.4 copy.195
  940.2 5.4 copy.198
  949.5 5.4 copy.201
  958.9 5.4 copy.204
  968.2 5.4 copy.207
  973.9 9.7 broadcast_in_dim.155
  983.6 9.0 scatter_fusion
  992.6 9.0 scatter_fusion.1
  1001.6 9.0 scatter_fusion.2
  1010.6 9.1 scatter_fusion.3
  1019.7 9.0 scatter_fusion.4
  1028.6 8.7 scatter_fusion.5
  1037.3 8.8 scatter_fusion.6
  1046.1 8.3 scatter_fusion.7
  1054.4 12.4 fusion.52
  1068.9 44.9 %collective-permute-start.6 = (f32[4,128,2048]{2,1,0:T(8,128)}, f32[4,128,2048]{2,1,0:T(8,128)}, u32[]{:S(2)}, u32[]{:S(2)}) collective-permute-start(f32[4,128,2048]{2,1,0:T(8,128)} %get-tuple-element.128), channel_id=1, source_target_pairs={{12,0},{16,4},{20,8},{24,12},{28,16},{32,20},{36,24},{40,28},{44,3... | collective-permute-start | bytes 12582920 | tf_op jit(solution)/shard_map/ppermute | solution.py:19
  1113.8 22.0 %collective-permute-start.5 = (f32[4,128,2048]{2,1,0:T(8,128)}, f32[4,128,2048]{2,1,0:T(8,128)}, u32[]{:S(2)}, u32[]{:S(2)}) collective-permute-start(f32[4,128,2048]{2,1,0:T(8,128)} %get-tuple-element.129), channel_id=1, source_target_pairs={{8,0},{12,4},{16,8},{20,12},{24,16},{28,20},{32,24},{36,28},{40,32... | collective-permute-start | bytes 12582920 | tf_op jit(solution)/shard_map/ppermute | solution.py:19
  1157.1 10.3 add_bitcast_fusion
  1172.0 92.0 %collective-permute-done.6 = f32[4,128,2048]{2,1,0:T(8,128)} collective-permute-done((f32[4,128,2048]{2,1,0:T(8,128)}, f32[4,128,2048]{2,1,0:T(8,128)}, u32[]{:S(2)}, u32[]{:S(2)}) %collective-permute-start.6) | collective-permute-done | bytes 4194336 | tf_op jit(solution)/shard_map/ppermute | solution.py:19
  1264.1 167.9 %collective-permute-done.5 = f32[4,128,2048]{2,1,0:T(8,128)} collective-permute-done((f32[4,128,2048]{2,1,0:T(8,128)}, f32[4,128,2048]{2,1,0:T(8,128)}, u32[]{:S(2)}, u32[]{:S(2)}) %collective-permute-start.5) | collective-permute-done | bytes 4194336 | tf_op jit(solution)/shard_map/ppermute | solution.py:19
  1432.0 10.4 fusion.5
  1442.4 6.6 reduce_sum.99
  (193 shorter events, 224.6 us)
Async XLA Ops:
  7.2 23.9 %copy-start.12 = (bf16[4,128,2048]{2,1,0:T(8,128)(2,1)S(1)}, bf16[4,128,2048]{2,1,0:T(8,128)(2,1)}, u32[]{:S(2)}) copy-start(bf16[4,128,2048]{2,1,0:T(8,128)(2,1)} %param.24) | copy-start | bytes 6291460
  7.2 1435.2 %all-gather.3.cloned.1.call-start = ((), (), s32[]{:S(2)}) async-start(), calls=%async_computation | async-start | bytes 16842752 | tf_op jit(solution)/shard_map/all_gather | solution.py:12
  7.2 47.1 %collective-permute-start = (bf16[4,128,2048]{2,1,0:T(8,128)(2,1)}, bf16[4,128,2048]{2,1,0:T(8,128)(2,1)}, u32[]{:S(2)}, u32[]{:S(2)}) collective-permute-start(bf16[4,128,2048]{2,1,0:T(8,128)(2,1)} %param.22), channel_id=1, source_target_pairs={{0,4},{4,8},{8,12},{12,16},{16,20},{20,24},{24,28},{28,32},{32,36}... | collective-permute-start | bytes 6291464 | tf_op jit(solution)/shard_map/ppermute | solution.py:19
  11.1 158.2 %collective-permute-start.1 = (bf16[4,128,2048]{2,1,0:T(8,128)(2,1)}, bf16[4,128,2048]{2,1,0:T(8,128)(2,1)}, u32[]{:S(2)}, u32[]{:S(2)}) collective-permute-start(bf16[4,128,2048]{2,1,0:T(8,128)(2,1)} %param.22), channel_id=1, source_target_pairs={{0,8},{4,12},{8,16},{12,20},{16,24},{20,28},{24,32},{28,36},{32,40... | collective-permute-start | bytes 6291464 | tf_op jit(solution)/shard_map/ppermute | solution.py:19
  14.3 160.1 %collective-permute-start.2 = (bf16[4,128,2048]{2,1,0:T(8,128)(2,1)}, bf16[4,128,2048]{2,1,0:T(8,128)(2,1)}, u32[]{:S(2)}, u32[]{:S(2)}) collective-permute-start(bf16[4,128,2048]{2,1,0:T(8,128)(2,1)} %param.22), channel_id=1, source_target_pairs={{0,12},{4,16},{8,20},{12,24},{16,28},{20,32},{24,36},{28,40},{32,4... | collective-permute-start | bytes 6291464 | tf_op jit(solution)/shard_map/ppermute | solution.py:19
  17.9 159.8 %collective-permute-start.3 = (bf16[4,128,2048]{2,1,0:T(8,128)(2,1)}, bf16[4,128,2048]{2,1,0:T(8,128)(2,1)}, u32[]{:S(2)}, u32[]{:S(2)}) collective-permute-start(bf16[4,128,2048]{2,1,0:T(8,128)(2,1)} %param.22), channel_id=1, source_target_pairs={{0,16},{4,20},{8,24},{12,28},{16,32},{20,36},{24,40},{28,44},{32,4... | collective-permute-start | bytes 6291464 | tf_op jit(solution)/shard_map/ppermute | solution.py:19
  30.5 0.6 copy-start.14
  33.5 9.5 copy-start.13
  37.6 7.0 copy-start.2
  37.6 7.0 copy-start.11
  394.2 15.6 %copy-start.16 = (f32[16,1024]{1,0:T(8,128)S(1)}, f32[16,1024]{1,0:T(8,128)}, u32[]{:S(2)}) copy-start(f32[16,1024]{1,0:T(8,128)} %param.25) | copy-start | bytes 196612
  968.2 5.4 copy-start.15
  1054.4 84.0 %copy-start = (bf16[16,8,128,128]{3,2,0,1:T(8,128)(2,1)S(1)}, bf16[16,8,128,128]{3,2,0,1:T(8,128)(2,1)}, u32[]{:S(2)}) copy-start(bf16[16,8,128,128]{3,2,0,1:T(8,128)(2,1)} %select_bitcast_fusion) | copy-start | bytes 12582916
  1054.4 84.0 %copy-start.4 = (bf16[4,1,128,2048]{2,3,0,1:T(8,128)(2,1)S(1)}, bf16[4,1,128,2048]{2,3,0,1:T(8,128)(2,1)}, u32[]{:S(2)}) copy-start(bf16[4,1,128,2048]{2,3,0,1:T(8,128)(2,1)} %copy.178) | copy-start | bytes 6291460
  1066.8 74.3 %copy-start.5 = (bf16[4,1,128,2048]{2,3,0,1:T(8,128)(2,1)S(1)}, bf16[4,1,128,2048]{2,3,0,1:T(8,128)(2,1)}, u32[]{:S(2)}) copy-start(bf16[4,1,128,2048]{2,3,0,1:T(8,128)(2,1)} %copy.176) | copy-start | bytes 6291460
  1066.8 105.2 %collective-permute-start.7 = (f32[4,128,2048]{2,1,0:T(8,128)}, f32[4,128,2048]{2,1,0:T(8,128)}, u32[]{:S(2)}, u32[]{:S(2)}) collective-permute-start(f32[4,128,2048]{2,1,0:T(8,128)} %get-tuple-element.127), channel_id=1, source_target_pairs={{16,0},{20,4},{24,8},{28,12},{32,16},{36,20},{40,24},{44,28},{48,3... | collective-permute-start | bytes 12582920 | tf_op jit(solution)/shard_map/ppermute | solution.py:19
  1068.9 195.2 %collective-permute-start.6 = (f32[4,128,2048]{2,1,0:T(8,128)}, f32[4,128,2048]{2,1,0:T(8,128)}, u32[]{:S(2)}, u32[]{:S(2)}) collective-permute-start(f32[4,128,2048]{2,1,0:T(8,128)} %get-tuple-element.128), channel_id=1, source_target_pairs={{12,0},{16,4},{20,8},{24,12},{28,16},{32,20},{36,24},{40,28},{44,3... | collective-permute-start | bytes 12582920 | tf_op jit(solution)/shard_map/ppermute | solution.py:19
  1113.8 318.1 %collective-permute-start.5 = (f32[4,128,2048]{2,1,0:T(8,128)}, f32[4,128,2048]{2,1,0:T(8,128)}, u32[]{:S(2)}, u32[]{:S(2)}) collective-permute-start(f32[4,128,2048]{2,1,0:T(8,128)} %get-tuple-element.129), channel_id=1, source_target_pairs={{8,0},{12,4},{16,8},{20,12},{24,16},{28,20},{32,24},{36,28},{40,32... | collective-permute-start | bytes 12582920 | tf_op jit(solution)/shard_map/ppermute | solution.py:19
  1135.8 296.2 %collective-permute-start.4 = (f32[4,128,2048]{2,1,0:T(8,128)}, f32[4,128,2048]{2,1,0:T(8,128)}, u32[]{:S(2)}, u32[]{:S(2)}) collective-permute-start(f32[4,128,2048]{2,1,0:T(8,128)} %get-tuple-element.126), channel_id=1, source_target_pairs={{4,0},{8,4},{12,8},{16,12},{20,16},{24,20},{28,24},{32,28},{36,32}... | collective-permute-start | bytes 12582920 | tf_op jit(solution)/shard_map/ppermute | solution.py:19
  1141.1 2.7 copy-start.6
  1143.8 2.7 copy-start.7
  1146.4 2.7 copy-start.8
  1149.1 2.6 copy-start.9
  1151.8 2.7 copy-start.10
  1154.4 2.7 copy-start.1
  1167.4 1.6 copy-start.3
Sparse Core Ops, SparseCore 0:
  410.0 186.3 all-gather.2
